TPU v7x, 32 devices: a whole 2x2x4 slice. The times are simulated.
32 devices in a mesh: seq: 4 (over y, x), dp: 8 (over z, core).
Axes of the slice: x: 2, y: 2, z: 4, core: 2. Of those that a mesh axis runs over, the one named last changes fastest.
Arguments:
- tokens: bfloat16 [16, 1024, 768], P('dp', 'seq'), may hold values from -6 to 6
- lengths: int32 [16], P('dp'), may hold values from 512 to 1024, as said below
- random_features: float32 [64, 256], replicated, may hold values from -6 to 6
- w_query: bfloat16 [768, 768], P(None, 'dp'), may hold values from -0.21875 to 0.21875
- w_key: bfloat16 [768, 768], P(None, 'dp'), may hold values from -0.21875 to 0.21875
- w_value: bfloat16 [768, 768], P(None, 'dp'), may hold values from -0.21875 to 0.21875
- w_output: bfloat16 [768, 768], P(None, 'dp'), may hold values from -3.5 to 3.5
- w_in: bfloat16 [768, 3072], P(None, 'dp'), may hold values from -0.21875 to 0.21875
- w_out: bfloat16 [3072, 768], P(None, 'dp'), may hold values from -0.109375 to 0.109375
- ln1_gain: bfloat16 [768], P('dp'), may hold values from 0.099609375 to 1.8984375
- ln1_bias: bfloat16 [768], P('dp'), may hold values from -3 to 3
- ln2_gain: bfloat16 [768], P('dp'), may hold values from 0.099609375 to 1.8984375
- ln2_bias: bfloat16 [768], P('dp'), may hold values from -3 to 3
- cotangent: bfloat16 [16, 1024, 768], P('dp', 'seq'), may hold values from -6 to 6
Outputs:
- layer_out: bfloat16 [16, 1024, 768], P('dp', 'seq')
- tokens_grad: float32 [16, 1024, 768], P('dp', 'seq')
- w_query_grad: float32 [768, 768], P(None, 'dp')
- w_key_grad: float32 [768, 768], P(None, 'dp')
- w_value_grad: float32 [768, 768], P(None, 'dp')
- w_output_grad: float32 [768, 768], P(None, 'dp')
- w_in_grad: float32 [768, 3072], P(None, 'dp')
- w_out_grad: float32 [3072, 768], P(None, 'dp')
- ln1_gain_grad: float32 [768], P('dp')
- ln1_bias_grad: float32 [768], P('dp')
- ln2_gain_grad: float32 [768], P('dp')
- ln2_bias_grad: float32 [768], P('dp')
Inputs may be any that keep to these rules, and one draw needn't show every extreme that they name: `lengths`: every sequence holds between 512 and 1024 valid tokens at its start; both ends occur.
All inputs are finite; a program needn't handle non-finite values.
Results may differ from a plain program's by a relative error of at most 0.015.
The roundings to bfloat16 on the way count: a program that leaves them out, or rounds other values in their place, can miss the bound.
Values may be sent and summed in bfloat16 or wider, within the bound.
A program may use at most 192 MiB of HBM per device.

v0:
```python
from functools import partial
import jax
import jax.numpy as jnp
from jax import lax
from jax.sharding import PartitionSpec as P

HEAD = 64
highest = lax.Precision.HIGHEST
norm_epsilon = 1e-12


def layer_norm(row_block, gain_vec, bias_vec):
    mean_val = jnp.mean(row_block, -1, keepdims=True)
    centered = row_block - mean_val
    inv_std = lax.rsqrt(jnp.mean(centered * centered, -1, keepdims=True) + norm_epsilon)
    normed = centered * inv_std
    return (normed * gain_vec + bias_vec, normed, inv_std)


def norm_back(grad_out, normed, inv_std, gain_vec):
    grad_normed = grad_out * gain_vec
    inner_term = (
        grad_normed
        - jnp.mean(grad_normed, -1, keepdims=True)
        - normed * jnp.mean(grad_normed * normed, -1, keepdims=True)
    )
    return (inv_std * inner_term, jnp.sum(grad_out * normed, 0), jnp.sum(grad_out, 0))


def row_product(left, right):
    return lax.dot_general(
        left, right, (((0,), (0,)), ((), ())), preferred_element_type=jnp.float32
    )


def feature_map(projected, random_features):
    scaled = projected.astype(jnp.float32) * HEAD ** (-0.25)
    projection = jnp.einsum("snhe,em->snhm", scaled, random_features, precision=highest)
    return (jnp.exp(projection - 0.5 * jnp.sum(scaled * scaled, -1, keepdims=True)), scaled)


def feature_back(grad_features, features, scaled, random_features):
    grad_proj = grad_features * features
    grad_scaled = jnp.einsum("snhm,em->snhe", grad_proj, random_features, precision=highest)
    grad_scaled = grad_scaled - scaled * jnp.sum(grad_proj, -1, keepdims=True)
    return grad_scaled * HEAD ** (-0.25)


def keep_local(key_state, key_total):
    return (key_state, key_total)


def mixer_forward(queries, key_proj, value_proj, key_mask, random_features, reducer):
    q_feat, q_scaled = feature_map(queries, random_features)
    k_feat, k_scaled = feature_map(key_proj, random_features)
    k_feat = k_feat * key_mask[:, :, None, None]
    key_state = jnp.einsum(
        "snhm,snhe->shme", k_feat, value_proj.astype(jnp.float32), precision=highest
    )
    key_total = jnp.sum(k_feat, 1)
    key_state, key_total = reducer(key_state, key_total)
    numerator = jnp.einsum("snhm,shme->snhe", q_feat, key_state, precision=highest)
    denominator = jnp.einsum("snhm,shm->snh", q_feat, key_total, precision=highest)
    context = numerator / denominator[..., None]
    return (
        context,
        (q_feat, q_scaled, k_feat, k_scaled, key_state, key_total, denominator, context),
    )


def mixer_backward(grad_context, value_proj, kept_mixer, random_features, reducer):
    q_feat, q_scaled, k_feat, k_scaled, key_state, key_total, denominator, context = kept_mixer
    grad_ctx = grad_context.astype(jnp.float32)
    grad_num = grad_ctx / denominator[..., None]
    grad_den = -jnp.sum(grad_ctx * context, -1) / denominator
    grad_qfeat = (
        jnp.einsum("snhe,shme->snhm", grad_num, key_state, precision=highest)
        + grad_den[..., None] * key_total[:, None]
    )
    grad_state = jnp.einsum("snhm,snhe->shme", q_feat, grad_num, precision=highest)
    grad_total = jnp.einsum("snhm,snh->shm", q_feat, grad_den, precision=highest)
    grad_state, grad_total = reducer(grad_state, grad_total)
    values_f32 = value_proj.astype(jnp.float32)
    grad_kfeat = (
        jnp.einsum("snhe,shme->snhm", values_f32, grad_state, precision=highest)
        + grad_total[:, None]
    )
    grad_values = jnp.einsum("snhm,shme->snhe", k_feat, grad_state, precision=highest)
    grad_queries = feature_back(grad_qfeat, q_feat, q_scaled, random_features)
    grad_keys = feature_back(grad_kfeat, k_feat, k_scaled, random_features)
    return (grad_queries, grad_keys, grad_values)


def shards(
    tokens,
    lengths,
    random_features,
    w_query,
    w_key,
    w_value,
    w_output,
    w_in,
    w_out,
    ln1_gain,
    ln1_bias,
    ln2_gain,
    ln2_bias,
    cotangent,
):
    seq_count, local_len, model_width = tokens.shape
    row_count = seq_count * local_len
    seq_parts = lax.axis_size("seq")
    heads_all = model_width // HEAD
    wq_full, wk_full, wv_full, wo_full, win_full, wout_full, gain1, bias1, gain2, bias2 = (
        lax.all_gather(w_query, "dp", axis=1, tiled=True),
        lax.all_gather(w_key, "dp", axis=1, tiled=True),
        lax.all_gather(w_value, "dp", axis=1, tiled=True),
        lax.all_gather(w_output, "dp", axis=1, tiled=True),
        lax.all_gather(w_in, "dp", axis=1, tiled=True),
        lax.all_gather(w_out, "dp", axis=1, tiled=True),
        lax.all_gather(ln1_gain, "dp", axis=0, tiled=True),
        lax.all_gather(ln1_bias, "dp", axis=0, tiled=True),
        lax.all_gather(ln2_gain, "dp", axis=0, tiled=True),
        lax.all_gather(ln2_bias, "dp", axis=0, tiled=True),
    )
    tok_rows = tokens.reshape(row_count, model_width)
    query_proj = jnp.dot(tok_rows, wq_full, preferred_element_type=jnp.float32).astype(jnp.bfloat16)
    key_proj = jnp.dot(tok_rows, wk_full, preferred_element_type=jnp.float32).astype(jnp.bfloat16)
    value_proj = jnp.dot(tok_rows, wv_full, preferred_element_type=jnp.float32).astype(jnp.bfloat16)
    local_pos = lax.axis_index("seq") * local_len + jnp.arange(local_len, dtype=jnp.int32)
    row_valid = (local_pos[None, :] < lengths[:, None]).astype(jnp.float32)
    full_len = local_len * seq_parts
    head_group = heads_all // seq_parts
    q_heads, k_heads, v_heads = (
        lax.all_to_all(
            query_proj.reshape(seq_count, local_len, model_width),
            "seq",
            split_axis=2,
            concat_axis=1,
            tiled=True,
        ),
        lax.all_to_all(
            key_proj.reshape(seq_count, local_len, model_width),
            "seq",
            split_axis=2,
            concat_axis=1,
            tiled=True,
        ),
        lax.all_to_all(
            value_proj.reshape(seq_count, local_len, model_width),
            "seq",
            split_axis=2,
            concat_axis=1,
            tiled=True,
        ),
    )
    q_heads = q_heads.reshape(seq_count, full_len, head_group, HEAD)
    k_heads = k_heads.reshape(seq_count, full_len, head_group, HEAD)
    v_heads = v_heads.reshape(seq_count, full_len, head_group, HEAD)
    full_pos = jnp.arange(full_len, dtype=jnp.int32)
    key_mask = (full_pos[None, :] < lengths[:, None]).astype(jnp.float32)
    context, kept_mixer = mixer_forward(
        q_heads, k_heads, v_heads, key_mask, random_features, keep_local
    )
    ctx_low = context.astype(jnp.bfloat16).reshape(seq_count, full_len, head_group * HEAD)
    ctx_tokens = lax.all_to_all(ctx_low, "seq", split_axis=1, concat_axis=2, tiled=True)
    ctx_rows = ctx_tokens.reshape(row_count, model_width)
    attn_out = jnp.dot(ctx_rows, wo_full, preferred_element_type=jnp.float32)
    resid1 = tok_rows.astype(jnp.float32) + attn_out
    hidden, normed1, inv1 = layer_norm(resid1, gain1.astype(jnp.float32), bias1.astype(jnp.float32))
    hidden_low = hidden.astype(jnp.bfloat16)
    pre_act = jnp.dot(hidden_low, win_full, preferred_element_type=jnp.float32)
    activated, gelu_pull = jax.vjp(partial(jax.nn.gelu, approximate=False), pre_act)
    act_low = activated.astype(jnp.bfloat16)
    ffn_out = jnp.dot(act_low, wout_full, preferred_element_type=jnp.float32)
    normed_out, normed2, inv2 = layer_norm(
        hidden + ffn_out, gain2.astype(jnp.float32), bias2.astype(jnp.float32)
    )
    valid_rows = row_valid.reshape(row_count, 1)
    layer_out = (
        (normed_out * valid_rows).astype(jnp.bfloat16).reshape(seq_count, local_len, model_width)
    )
    wq_back, wk_back, wv_back, wo_back, win_back, wout_back, gain1_back, gain2_back = (
        lax.all_gather(w_query, "dp", axis=1, tiled=True),
        lax.all_gather(w_key, "dp", axis=1, tiled=True),
        lax.all_gather(w_value, "dp", axis=1, tiled=True),
        lax.all_gather(w_output, "dp", axis=1, tiled=True),
        lax.all_gather(w_in, "dp", axis=1, tiled=True),
        lax.all_gather(w_out, "dp", axis=1, tiled=True),
        lax.all_gather(ln1_gain, "dp", axis=0, tiled=True),
        lax.all_gather(ln2_gain, "dp", axis=0, tiled=True),
    )
    grad_y = cotangent.reshape(row_count, model_width).astype(jnp.float32) * valid_rows
    grad_r2, grad_gain2, grad_bias2 = norm_back(
        grad_y, normed2, inv2, gain2_back.astype(jnp.float32)
    )
    grad_ffn = grad_r2.astype(jnp.bfloat16)
    grad_wout = row_product(act_low, grad_ffn)
    grad_act = lax.dot_general(
        grad_ffn, wout_back, (((1,), (1,)), ((), ())), preferred_element_type=jnp.float32
    )
    grad_pre = gelu_pull(grad_act)[0].astype(jnp.bfloat16)
    grad_win = row_product(hidden_low, grad_pre)
    grad_hidden = grad_r2 + lax.dot_general(
        grad_pre, win_back, (((1,), (1,)), ((), ())), preferred_element_type=jnp.float32
    )
    grad_r1, grad_gain1, grad_bias1 = norm_back(
        grad_hidden, normed1, inv1, gain1_back.astype(jnp.float32)
    )
    grad_attn = grad_r1.astype(jnp.bfloat16)
    grad_wo = row_product(ctx_rows, grad_attn)
    grad_ctx = lax.dot_general(
        grad_attn, wo_back, (((1,), (1,)), ((), ())), preferred_element_type=jnp.float32
    ).astype(jnp.bfloat16)
    grad_heads = lax.all_to_all(
        grad_ctx.reshape(seq_count, local_len, model_width),
        "seq",
        split_axis=2,
        concat_axis=1,
        tiled=True,
    )
    grad_heads = grad_heads.reshape(seq_count, full_len, head_group, HEAD)
    grad_q, grad_k, grad_v = mixer_backward(
        grad_heads, v_heads, kept_mixer, random_features, keep_local
    )
    grad_q_tok, grad_k_tok, grad_v_tok = (
        lax.all_to_all(
            grad_q.astype(jnp.bfloat16).reshape(seq_count, full_len, head_group * HEAD),
            "seq",
            split_axis=1,
            concat_axis=2,
            tiled=True,
        ),
        lax.all_to_all(
            grad_k.astype(jnp.bfloat16).reshape(seq_count, full_len, head_group * HEAD),
            "seq",
            split_axis=1,
            concat_axis=2,
            tiled=True,
        ),
        lax.all_to_all(
            grad_v.astype(jnp.bfloat16).reshape(seq_count, full_len, head_group * HEAD),
            "seq",
            split_axis=1,
            concat_axis=2,
            tiled=True,
        ),
    )
    grad_q_rows = grad_q_tok.reshape(row_count, model_width)
    grad_k_rows = grad_k_tok.reshape(row_count, model_width)
    grad_v_rows = grad_v_tok.reshape(row_count, model_width)
    grad_wq = row_product(tok_rows, grad_q_rows)
    grad_wk = row_product(tok_rows, grad_k_rows)
    grad_wv = row_product(tok_rows, grad_v_rows)
    contract_out = (((1,), (1,)), ((), ()))
    grad_tokens = grad_r1 + lax.dot_general(
        grad_q_rows, wq_back, contract_out, preferred_element_type=jnp.float32
    )
    grad_tokens = grad_tokens + lax.dot_general(
        grad_k_rows, wk_back, contract_out, preferred_element_type=jnp.float32
    )
    grad_tokens = grad_tokens + lax.dot_general(
        grad_v_rows, wv_back, contract_out, preferred_element_type=jnp.float32
    )
    (
        share_wq,
        share_wk,
        share_wv,
        share_wo,
        share_win,
        share_wout,
        share_g1,
        share_b1,
        share_g2,
        share_b2,
    ) = (
        lax.psum_scatter(grad_wq, "dp", scatter_dimension=1, tiled=True),
        lax.psum_scatter(grad_wk, "dp", scatter_dimension=1, tiled=True),
        lax.psum_scatter(grad_wv, "dp", scatter_dimension=1, tiled=True),
        lax.psum_scatter(grad_wo, "dp", scatter_dimension=1, tiled=True),
        lax.psum_scatter(grad_win, "dp", scatter_dimension=1, tiled=True),
        lax.psum_scatter(grad_wout, "dp", scatter_dimension=1, tiled=True),
        lax.psum_scatter(grad_gain1, "dp", scatter_dimension=0, tiled=True),
        lax.psum_scatter(grad_bias1, "dp", scatter_dimension=0, tiled=True),
        lax.psum_scatter(grad_gain2, "dp", scatter_dimension=0, tiled=True),
        lax.psum_scatter(grad_bias2, "dp", scatter_dimension=0, tiled=True),
    )
    (
        final_wq,
        final_wk,
        final_wv,
        final_wo,
        final_win,
        final_wout,
        final_g1,
        final_b1,
        final_g2,
        final_b2,
    ) = (
        lax.psum(share_wq.astype(jnp.bfloat16), "seq").astype(jnp.float32),
        lax.psum(share_wk.astype(jnp.bfloat16), "seq").astype(jnp.float32),
        lax.psum(share_wv.astype(jnp.bfloat16), "seq").astype(jnp.float32),
        lax.psum(share_wo.astype(jnp.bfloat16), "seq").astype(jnp.float32),
        lax.psum(share_win.astype(jnp.bfloat16), "seq").astype(jnp.float32),
        lax.psum(share_wout.astype(jnp.bfloat16), "seq").astype(jnp.float32),
        lax.psum(share_g1.astype(jnp.bfloat16), "seq").astype(jnp.float32),
        lax.psum(share_b1.astype(jnp.bfloat16), "seq").astype(jnp.float32),
        lax.psum(share_g2.astype(jnp.bfloat16), "seq").astype(jnp.float32),
        lax.psum(share_b2.astype(jnp.bfloat16), "seq").astype(jnp.float32),
    )
    return (
        layer_out,
        grad_tokens.reshape(seq_count, local_len, model_width),
        final_wq,
        final_wk,
        final_wv,
        final_wo,
        final_win,
        final_wout,
        final_g1,
        final_b1,
        final_g2,
        final_b2,
    )


def solution(mesh):
    in_specs = (
        P("dp", "seq", None),
        P("dp"),
        P(),
        P(None, "dp"),
        P(None, "dp"),
        P(None, "dp"),
        P(None, "dp"),
        P(None, "dp"),
        P(None, "dp"),
        P("dp"),
        P("dp"),
        P("dp"),
        P("dp"),
        P("dp", "seq", None),
    )
    out_specs = (
        P("dp", "seq", None),
        P("dp", "seq", None),
        P(None, "dp"),
        P(None, "dp"),
        P(None, "dp"),
        P(None, "dp"),
        P(None, "dp"),
        P(None, "dp"),
        P("dp"),
        P("dp"),
        P("dp"),
        P("dp"),
    )
    return jax.shard_map(shards, mesh=mesh, in_specs=in_specs, out_specs=out_specs, check_vma=False)
```

profile of v0, /device:TPU:0, one launch (start us, length us, event | category | flops | bytes accessed | tf_op | source)
XLA Modules:
  0.0 704.7 jit_solution(9426483692324572481)
XLA Ops:
  10.6 24.6 %all-gather.7.cloned.1.call-done = bf16[768,768]{0,1:T(8,128)(2,1)} async-done(((bf16[768,96]{0,1:T(8,128)(2,1)}), bf16[768,768]{0,1:T(8,128)(2,1)}) %all-gather.7.cloned.1.call-update) | async-done | bytes 1179664 | tf_op jit(solution)/shard_map/all_gather | solution.py:116
  43.5 15.9 %all-gather.11.cloned.1.call-done = bf16[768,768]{0,1:T(8,128)(2,1)} async-done(((bf16[768,96]{0,1:T(8,128)(2,1)}), bf16[768,768]{0,1:T(8,128)(2,1)}) %all-gather.11.cloned.1.call-update) | async-done | bytes 1179664 | tf_op jit(solution)/shard_map/all_gather | solution.py:115
  63.3 4.2 all-to-all-start.2
  69.8 16.1 %all-reduce.9 = (bf16[768]{0:T(1024)(128)(2,1)S(1)}, bf16[768]{0:T(1024)(128)(2,1)S(1)}, bf16[768]{0:T(1024)(128)(2,1)S(1)}, bf16[768]{0:T(1024)(128)(2,1)S(1)}) all-reduce(bf16[768]{0:T(1024)(128)(2,1)S(1)} %dynamic-update-slice.1, bf16[768]{0:T(1024)(128)(2,1)S(1)} %dynamic-update-slice, ...), channel_id=1, replica_groups=mesh['seq'=4,'dp'=8] {'dp'}, use_global_device_ids=true, to_apply=%add.1 | all-reduce | flops 3072 | bytes 12288
  91.9 4.4 all-to-all-start.1
  111.0 7.3 %fusion.20 = f32[2,1024,3,256]{1,3,2,0:T(8,128)S(1)} fusion(f32[2,1024,3,64]{1,3,2,0:T(8,128)S(1)} %reshape.237, f32[64,256]{1,0:T(8,128)S(1)} %copy-done), kind=kOutput, calls=%fused_computation.64 | convolution fusion | flops 1208352768 | bytes 7929856 | tf_op jit(solution)/shard_map/snhe,em->snhm/dot_general | solution.py:38
  118.4 7.2 %fusion.16 = (f32[2,3,256]{2,1,0:T(4,128)S(1)}, f32[2,1024,3,256]{3,1,2,0:T(8,128)S(1)}) fusion(f32[2,1024]{1,0:T(2,128)S(1)} %compare_convert_fusion, f32[2,1024,3]{1,2,0:T(4,128)S(1)} %broadcast_multiply_fusion.3, f32[64,256]{1,0:T(8,128)S(1)} %copy-done, f32[2,1024,3,64]{1,3,2,0:T(8,128)S(1)} %reshape.236), kind=kOutput, calls=%fused_computation.31 | convolution fusion | flops 1213069824 | bytes 7968768 | tf_op jit(solution)/shard_map/snhe,em->snhm/dot_general | solution.py:38
  132.9 5.6 fusion.52
  144.6 12.6 %all-to-all-done.3 = bf16[2,1024,192]{2,0,1:T(2,128)(2,1)S(1)} async-done(((bf16[2,1024,192]{2,0,1:T(2,128)(2,1)}), bf16[2,1024,192]{2,0,1:T(2,128)(2,1)S(1)}, u32[]{:S(2)}, u32[]{:S(2)}) %all-to-all-start.3) | async-done | bytes 786464 | tf_op jit(solution)/shard_map/all_to_all | solution.py:166
  169.2 20.7 %multiply_convert_fusion = (bf16[512,3072]{1,0:T(8,128)(2,1)}, f32[512,3072]{1,0:T(8,128)}, f32[512,3072]{1,0:T(8,128)}) fusion(bf16[768,3072]{1,0:T(8,128)(2,1)} %all-gather.15.cloned.1.call-done, f32[512,768]{1,0:T(8,128)} %copy-done.21, f32[768]{0:T(1024)S(1)} %convert_element_type.205, f32[768]{0:T(1024)S(1)} %convert_element_type.204, ...), kind=kOutput, calls=%fused_computation.6 | convolution fusion | flops 2520121344 | bytes 22030336 | tf_op jit(solution)/shard_map/dot_general | solution.py:172
  190.0 21.4 %all-gather.17.cloned.1.call-done = bf16[3072,768]{0,1:T(8,128)(2,1)} async-done(((bf16[3072,96]{0,1:T(8,128)(2,1)}), bf16[3072,768]{0,1:T(8,128)(2,1)}) %all-gather.17.cloned.1.call-update) | async-done | bytes 4718608 | tf_op jit(solution)/shard_map/all_gather | solution.py:120
  211.4 6.6 fusion.54
  220.7 7.7 %add_convert_fusion = bf16[512,3072]{1,0:T(8,128)(2,1)S(1)} fusion(f32[512,3072]{1,0:T(8,128)S(1)} %copy-done.41, f32[512,3072]{1,0:T(8,128)} %get-tuple-element.52, bf16[3072,768]{0,1:T(8,128)(2,1)S(1)} %copy-done.33, f32[512,768]{1,0:T(8,128)S(1)} %get-tuple-element.40), kind=kOutput, calls=%fused_computation.5 | convolution fusion | flops 2438332416 | bytes 22020096 | tf_op jit(solution)/shard_map/dot_general | solution.py:199
  240.3 15.4 %all_to_all.102 = bf16[2,256,768]{1,0,2:T(2,128)(2,1)S(1)} all-to-all(bf16[2,256,768]{1,0,2:T(2,128)(2,1)S(1)} %copy.73), channel_id=1, replica_groups=mesh['seq'=4,'dp'=8] {'seq'}, dimensions={2} | all-to-all | bytes 1572864 | tf_op jit(solution)/shard_map/all_to_all | solution.py:215
  261.1 10.2 %fusion.8 = f32[2,3,256,64]{2,3,1,0:T(8,128)S(1)} fusion(f32[2,1024,3,256]{1,3,2,0:T(8,128)} %copy-done.1, f32[2,1024,3]{1,2,0:T(4,128)S(1)} %broadcast_multiply_fusion.2, f32[2,1024,3,64]{1,3,2,0:T(8,128)} %reshape.240, f32[2,1024,3]{1,2,0:T(4,128)S(1)} %bitcast.205), kind=kOutput, calls=%fused_computation.23 | convolution fusion | flops 1209925632 | bytes 8306688 | tf_op jit(solution)/shard_map/snhm,snhe->shme/dot_general | solution.py:80
  271.3 7.8 %fusion.24 = bf16[2,3,64,1024]{3,2,1,0:T(8,128)(2,1)} fusion(f32[2,3,256,64]{2,3,1,0:T(8,128)S(1)} %fusion.8, f32[2,1024,3,256]{3,1,2,0:T(8,128)S(1)} %bitcast.160, f32[2,1024]{1,0:T(2,128)S(1)} %compare_convert_fusion, f32[2,1024,3]{1,2,0:T(4,128)S(1)} %broadcast_multiply_fusion.3), kind=kOutput, calls=%fused_computation.74 | convolution fusion | flops 1211498496 | bytes 7503872 | tf_op jit(solution)/shard_map/snhm,shme->snhe/dot_general | solution.py:88
  281.6 15.8 %all_to_all.103 = bf16[2,1024,192]{2,0,1:T(2,128)(2,1)S(1)} all-to-all(bf16[2,1024,192]{2,0,1:T(2,128)(2,1)S(1)} %copy.85), channel_id=1, replica_groups=mesh['seq'=4,'dp'=8] {'seq'}, dimensions={1} | all-to-all | bytes 1572864 | tf_op jit(solution)/shard_map/all_to_all | solution.py:241
  306.0 8.4 %fusion.7 = f32[2,3,1,256]{3,2,1,0:T(1,128)S(1)} fusion(f32[2,1024,3,256]{1,3,2,0:T(8,128)} %copy-done.1, f32[2,1024,3]{1,2,0:T(4,128)S(1)} %broadcast_multiply_fusion.2, f32[2,1024,3,1]{1,2,0,3:T(4,128)S(1)} %bitcast.207), kind=kOutput, calls=%fused_computation.22 | convolution fusion | flops 20447232 | bytes 6346752 | tf_op jit(solution)/shard_map/snhm,snh->shm/dot_general | solution.py:81
  314.5 4.8 fusion.55
  319.4 6.2 multiply_convert_fusion.1
  326.5 14.7 %all_to_all.104 = bf16[2,1024,192]{2,0,1:T(2,128)(2,1)S(1)} all-to-all(bf16[2,1024,192]{2,0,1:T(2,128)(2,1)S(1)} %copy.82), channel_id=1, replica_groups=mesh['seq'=4,'dp'=8] {'seq'}, dimensions={1} | all-to-all | bytes 1572864 | tf_op jit(solution)/shard_map/all_to_all | solution.py:234
  347.4 11.6 %fusion.56 = (f32[2,1024,3]{1,2,0:T(4,128)S(1)}, f32[2,1024,3,256]{1,3,2,0:T(8,128)S(1)}) fusion(f32[2,1024,3,256]{1,3,2,0:T(8,128)} %copy-done.1, f32[2,1024,3]{1,2,0:T(4,128)S(1)} %broadcast_multiply_fusion.2, f32[2,3,256]{2,1,0:T(4,128)S(1)} %get-tuple-element.46, f32[2,1024,3]{1,2,0:T(4,128)S(1)} %negate_divide_fusion, ...), kind=kOutput, calls=%fused_computation.125 | convolution fusion | flops 1216210944 | bytes 14653440 | tf_op jit(solution)/shard_map/snhe,shme->snhm/dot_general | solution.py:77
  359.1 4.3 multiply_convert_fusion.2
  364.3 13.4 %all_to_all.105 = bf16[2,1024,192]{2,0,1:T(2,128)(2,1)S(1)} all-to-all(bf16[2,1024,192]{2,0,1:T(2,128)(2,1)S(1)} %copy.77), channel_id=1, replica_groups=mesh['seq'=4,'dp'=8] {'seq'}, dimensions={1} | all-to-all | bytes 1572864 | tf_op jit(solution)/shard_map/all_to_all | solution.py:227
  382.9 7.2 %fusion.46 = f32[768,3072]{1,0:T(8,128)} fusion(bf16[512,3072]{1,0:T(8,128)(2,1)} %copy-done.40, f32[512,768]{1,0:T(8,128)S(1)} %copy-done.23, f32[768]{0:T(1024)S(1)} %convert_element_type.205, f32[768]{0:T(1024)S(1)} %convert_element_type.204, f32[512]{0:T(512)S(1)} %add_rsqrt_fusion.1, f32[512]{0:T(512)S(1)} %broadcast_multiply_fusion.8), kind=kOutput, calls=%fused_computation.118 | convolution fusion | flops 2417885184 | bytes 14166016 | tf_op jit(solution)/shard_map/dot_general | solution.py:31
  391.5 7.0 fusion.31
  403.5 16.4 %reduce-scatter.7.cloned.1.call-done = f32[768,96]{0,1:T(8,128)} async-done(((f32[768,768]{0,1:T(8,128)}), f32[768,96]{0,1:T(8,128)}) %reduce-scatter.7.cloned.1.call-update) | async-done | bytes 294928 | tf_op jit(solution)/shard_map/reduce_scatter | solution.py:277
  421.5 98.9 %reduce-scatter.15.cloned.1.call-done = f32[768,384]{1,0:T(8,128)} async-done(((f32[768,3072]{1,0:T(8,128)}), f32[768,384]{1,0:T(8,128)}) %reduce-scatter.15.cloned.1.call-update) | async-done | bytes 1179664 | tf_op jit(solution)/shard_map/reduce_scatter | solution.py:281
  522.6 97.9 %reduce-scatter.17.cloned.1.call-done = f32[3072,96]{0,1:T(8,128)} async-done(((f32[3072,768]{0,1:T(8,128)}), f32[3072,96]{0,1:T(8,128)}) %reduce-scatter.17.cloned.1.call-update) | async-done | bytes 1179664 | tf_op jit(solution)/shard_map/reduce_scatter | solution.py:282
  623.4 25.9 %all-reduce.8 = (bf16[768]{0:T(1024)(128)(2,1)S(1)}, bf16[768]{0:T(1024)(128)(2,1)S(1)}, bf16[768]{0:T(1024)(128)(2,1)S(1)}, bf16[768]{0:T(1024)(128)(2,1)S(1)}) all-reduce(f32[768]{0:T(1024)S(1)} %get-tuple-element.12, f32[768]{0:T(1024)S(1)} %get-tuple-element.17, ...), channel_id=8, replica_groups=mesh['seq'=4,'dp'=8] {'dp'}, use_global_device_ids=true, to_apply=%region_27.0.clone | all-reduce | flops 3072 | bytes 18432
  649.6 9.9 %all-reduce.10 = (bf16[96]{0:T(256)(128)(2,1)S(1)}, bf16[96]{0:T(256)(128)(2,1)S(1)}, bf16[96]{0:T(256)(128)(2,1)S(1)}, bf16[96]{0:T(256)(128)(2,1)S(1)}) all-reduce(bf16[96]{0:T(256)(128)(2,1)S(1)} %dynamic-slice.19, bf16[96]{0:T(256)(128)(2,1)S(1)} %dynamic-slice.18, ...), channel_id=1, replica_groups=mesh['seq'=4,'dp'=8] {'seq'}, use_global_device_ids=true, to_apply=%region_28.0 | all-reduce | flops 384 | bytes 1536 | tf_op jit(solution)/shard_map/psum | solution.py:306
  667.3 20.8 %all-reduce.14.cloned.1.call-done = (bf16[768,96]{0,1:T(8,128)(2,1)}, bf16[768,96]{0,1:T(8,128)(2,1)}, bf16[768,96]{0,1:T(8,128)(2,1)}, bf16[768,96]{0,1:T(8,128...) async-done(((bf16[768,96]{0,1:T(8,128)(2,1)}, bf16[768,96]{0,1:T(8,128)(2,1)}, bf16[768,96]{0,1:T(8,128)(2,1)}, bf16[768,96]{0,1:T(8,128)(2,1)}, ...) | async-done | bytes 1769488 | tf_op jit(solution)/shard_map/psum | solution.py:300
  (247 shorter events, 137.2 us)
Async XLA Ops:
  7.2 103.8 %copy-start = (f32[64,256]{1,0:T(8,128)S(1)}, f32[64,256]{1,0:T(8,128)}, u32[]{:S(2)}) copy-start(f32[64,256]{1,0:T(8,128)} %param.16) | copy-start | bytes 196612
  7.2 28.0 %all-gather.7.cloned.1.call-start = ((), (), s32[]{:S(2)}) async-start(), calls=%async_computation.14 | async-start | bytes 1327104 | tf_op jit(solution)/shard_map/all_gather | solution.py:116
  7.9 51.4 %all-gather.11.cloned.1.call-start = ((), (), s32[]{:S(2)}) async-start(), calls=%async_computation.16 | async-start | bytes 1327104 | tf_op jit(solution)/shard_map/all_gather | solution.py:115
  8.7 77.2 %all-gather.9.cloned.1.call-start = ((), (), s32[]{:S(2)}) async-start(), calls=%async_computation.15 | async-start | bytes 1327104 | tf_op jit(solution)/shard_map/all_gather | solution.py:117
  9.4 155.9 %all-gather.13.cloned.1.call-start = ((), (), s32[]{:S(2)}) async-start(), calls=%async_computation.17 | async-start | bytes 1327104 | tf_op jit(solution)/shard_map/all_gather | solution.py:118
  10.0 159.2 %all-gather.15.cloned.1.call-start = ((), (), s32[]{:S(2)}) async-start(), calls=%async_computation.18 | async-start | bytes 5308416 | tf_op jit(solution)/shard_map/all_gather | solution.py:119
  37.5 21.9 %copy-start.12 = (bf16[2,256,768]{2,1,0:T(8,128)(2,1)S(1)}, bf16[2,256,768]{2,1,0:T(8,128)(2,1)}, u32[]{:S(2)}) copy-start(bf16[2,256,768]{2,1,0:T(8,128)(2,1)} %param.14) | copy-start | bytes 2359300
  39.3 24.0 %all-to-all-start = ((bf16[2,256,768]{1,0,2:T(2,128)(2,1)}), bf16[2,256,768]{1,0,2:T(2,128)(2,1)S(1)}, u32[]{:S(2)}, u32[]{:S(2)}) async-start(bf16[2,256,768]{1,0,2:T(2,128)(2,1)} %copy.60), calls=%async_computation | async-start | bytes 1572864 | tf_op jit(solution)/shard_map/all_to_all | solution.py:142
  42.9 168.5 %all-gather.17.cloned.1.call-start = ((), (), s32[]{:S(2)}) async-start(), calls=%async_computation.19 | async-start | bytes 5308416 | tf_op jit(solution)/shard_map/all_gather | solution.py:120
  61.5 8.0 %copy-start.39 = (bf16[96]{0:T(256)(128)(2,1)S(1)}, bf16[96]{0:T(256)(128)(2,1)}, u32[]{:S(2)}) copy-start(bf16[96]{0:T(256)(128)(2,1)} %param.25) | copy-start | bytes 580
  63.3 28.6 %all-to-all-start.2 = ((bf16[2,256,768]{1,0,2:T(2,128)(2,1)}), bf16[2,256,768]{1,0,2:T(2,128)(2,1)}, u32[]{:S(2)}, u32[]{:S(2)}) async-start(bf16[2,256,768]{1,0,2:T(2,128)(2,1)} %copy.66), calls=%async_computation.2 | async-start | bytes 1572864 | tf_op jit(solution)/shard_map/all_to_all | solution.py:135
  91.9 26.5 %copy-start.3 = (f32[2,1024,3,64]{1,3,2,0:T(8,128)}, f32[2,1024,3,64]{1,3,2,0:T(8,128)S(1)}, u32[]{:S(2)}) copy-start(f32[2,1024,3,64]{1,3,2,0:T(8,128)S(1)} %reshape.236) | copy-start | bytes 4718596
  91.9 13.8 %all-to-all-start.1 = ((bf16[2,256,768]{1,0,2:T(2,128)(2,1)}), bf16[2,256,768]{1,0,2:T(2,128)(2,1)}, u32[]{:S(2)}, u32[]{:S(2)}) async-start(bf16[2,256,768]{1,0,2:T(2,128)(2,1)} %copy.63), calls=%async_computation.1 | async-start | bytes 1572864 | tf_op jit(solution)/shard_map/all_to_all | solution.py:149
  101.9 9.1 %copy-start.5 = (f32[2,1024,3,64]{1,3,2,0:T(8,128)}, f32[2,1024,3,64]{1,3,2,0:T(8,128)S(1)}, u32[]{:S(2)}) copy-start(f32[2,1024,3,64]{1,3,2,0:T(8,128)S(1)} %reshape.237) | copy-start | bytes 4718596
  118.4 14.5 %copy-start.1 = (f32[2,1024,3,256]{1,3,2,0:T(8,128)}, f32[2,1024,3,256]{1,3,2,0:T(8,128)S(1)}, u32[]{:S(2)}) copy-start(f32[2,1024,3,256]{1,3,2,0:T(8,128)S(1)} %fusion.20) | copy-start | bytes 18874372
  140.4 16.7 %all-to-all-start.3 = ((bf16[2,1024,192]{2,0,1:T(2,128)(2,1)}), bf16[2,1024,192]{2,0,1:T(2,128)(2,1)S(1)}, u32[]{:S(2)}, u32[]{:S(2)}) async-start(bf16[2,1024,192]{2,0,1:T(2,128)(2,1)} %copy.70), calls=%async_computation.3 | async-start | bytes 2097152 | tf_op jit(solution)/shard_map/all_to_all | solution.py:166
  144.0 254.6 %reduce-scatter.13.cloned.1.call-start = ((), (), s32[]{:S(2)}) async-start(), calls=%async_computation.23 | async-start | bytes 2654208 | tf_op jit(solution)/shard_map/reduce_scatter | solution.py:280
  211.4 9.3 %copy-start.41 = (f32[512,3072]{1,0:T(8,128)S(1)}, f32[512,3072]{1,0:T(8,128)}, u32[]{:S(2)}) copy-start(f32[512,3072]{1,0:T(8,128)} %get-tuple-element.39) | copy-start | bytes 18874372
  219.1 9.3 %slice-start.4 = ((s8[4718592]{0:T(1024)(128)(4,1)}), s8[4194304]{0:T(1024)(128)(4,1)S(1)}, s32[]{:S(2)}) async-start(s8[4718592]{0:T(1024)(128)(4,1)} %bitcast.213), calls=%async_computation.31 | async-start | bytes 8388608
  234.9 165.3 %reduce-scatter.11.cloned.1.call-start = ((), (), s32[]{:S(2)}) async-start(), calls=%async_computation.22 | async-start | bytes 2654208 | tf_op jit(solution)/shard_map/reduce_scatter | solution.py:279
  258.0 13.3 %slice-start = ((s8[6291456]{0:T(1024)(128)(4,1)}), s8[2097152]{0:T(1024)(128)(4,1)S(1)}, s32[]{:S(2)}) async-start(s8[6291456]{0:T(1024)(128)(4,1)} %bitcast.159), calls=%async_computation.27 | async-start | bytes 4194304
  261.1 10.2 %slice-start.1 = ((s8[6291456]{0:T(1024)(128)(4,1)}), s8[4194304]{0:T(1024)(128)(4,1)S(1)}, s32[]{:S(2)}) async-start(s8[6291456]{0:T(1024)(128)(4,1)} %bitcast.159), calls=%async_computation.28 | async-start | bytes 8388608
  301.3 13.2 %slice-start.2 = ((s8[6291456]{0:T(1024)(128)(4,1)}), s8[2097152]{0:T(1024)(128)(4,1)S(1)}, s32[]{:S(2)}) async-start(s8[6291456]{0:T(1024)(128)(4,1)} %bitcast.161), calls=%async_computation.29 | async-start | bytes 4194304
  303.6 98.3 %reduce-scatter.9.cloned.1.call-start = ((), (), s32[]{:S(2)}) async-start(), calls=%async_computation.21 | async-start | bytes 2654208 | tf_op jit(solution)/shard_map/reduce_scatter | solution.py:278
  303.6 10.9 %slice-start.3 = ((s8[6291456]{0:T(1024)(128)(4,1)}), s8[4194304]{0:T(1024)(128)(4,1)S(1)}, s32[]{:S(2)}) async-start(s8[6291456]{0:T(1024)(128)(4,1)} %bitcast.161), calls=%async_computation.30 | async-start | bytes 8388608
  347.3 11.7 %copy-start.6 = (f32[2,1024,3,64]{1,3,2,0:T(8,128)S(1)}, f32[2,1024,3,64]{1,3,2,0:T(8,128)}, u32[]{:S(2)}) copy-start(f32[2,1024,3,64]{1,3,2,0:T(8,128)} %copy-done.5) | copy-start | bytes 4718596
  347.3 72.5 %reduce-scatter.7.cloned.1.call-start = ((), (), s32[]{:S(2)}) async-start(), calls=%async_computation.20 | async-start | bytes 2654208 | tf_op jit(solution)/shard_map/reduce_scatter | solution.py:277
  382.8 137.7 %reduce-scatter.15.cloned.1.call-start = ((), (), s32[]{:S(2)}) async-start(), calls=%async_computation.24 | async-start | bytes 10616832 | tf_op jit(solution)/shard_map/reduce_scatter | solution.py:281
  390.1 230.4 %reduce-scatter.17.cloned.1.call-start = ((), (), s32[]{:S(2)}) async-start(), calls=%async_computation.25 | async-start | bytes 10616832 | tf_op jit(solution)/shard_map/reduce_scatter | solution.py:282
  398.5 289.5 %all-reduce.14.cloned.1.call-start = ((), (), s32[]{:S(2)}) async-start(), calls=%async_computation.26 | async-start | bytes 3538944 | tf_op jit(solution)/shard_map/psum | solution.py:300
  421.5 240.1 %copy-start.35 = (bf16[768,768]{0,1:T(8,128)(2,1)S(1)}, bf16[768,768]{0,1:T(8,128)(2,1)}, u32[]{:S(2)}) copy-start(bf16[768,768]{0,1:T(8,128)(2,1)} %all-gather.11.cloned.1.call-done) | copy-start | bytes 3538948
  688.0 8.8 %copy-start.30 = (bf16[3072,96]{0,1:T(8,128)(2,1)S(1)}, bf16[3072,96]{0,1:T(8,128)(2,1)}, u32[]{:S(2)}) copy-start(bf16[3072,96]{0,1:T(8,128)(2,1)} %get-tuple-element.37) | copy-start | bytes 1769476
  (33 other events, 123.8 us)
Sparse Core Ops, SparseCore 0:
  9.6 25.4 all-gather.6
  36.8 22.5 all-gather.10
  61.0 22.6 all-gather.8
  85.2 22.2 all-gather.12
  108.9 51.0 all-gather.14
  161.5 49.8 all-gather.16
  235.1 35.7 reduce-scatter.12
  303.7 34.1 reduce-scatter.10
  347.5 34.1 reduce-scatter.8
  383.8 36.0 reduce-scatter.6
  422.2 98.2 reduce-scatter.14
  522.6 97.8 reduce-scatter.16
  624.9 63.0 all-reduce.13
where the time goes:
time: 711 us; the launch traced here: 705 us
  waiting for transfers between devices  316 us (44%)
  matrix products  158 us (22%)
  blocking collectives  111 us (16%)
  local copies, waits for them, and re-layouts  57.7 us (8%)
  other arithmetic  30.1 us (4%)
  between operations  16.4 us (2%)
  starting transfers between devices  16.1 us (2%)
    reduce_scatter x1, waiting for transfers between devices, shards(): lax.psum_scatter(grad_win, 'dp', scatter_dimension=1, tiled=True)  98.9 us
    reduce_scatter x1, waiting for transfers between devices, shards(): lax.psum_scatter(grad_wout, 'dp', scatter_dimension=1, tiled=True)  97.9 us
    unnamed x2, blocking collectives  42 us
    all_gather x1, waiting for transfers between devices, shards(): lax.all_gather(w_key, 'dp', axis=1, tiled=True)  24.6 us
    dot_general x6, matrix products, row_product(): lax.dot_general(left, right, (((0,), (0,)), ((), ())), preferred_element_...  23.1 us
    all_gather x1, waiting for transfers between devices, shards(): lax.all_gather(w_out, 'dp', axis=1, tiled=True)  21.4 us
    psum x1, waiting for transfers between devices, shards(): lax.psum(share_wq.astype(jnp.bfloat16), 'seq').astype(jnp.float32)  20.8 us
    dot_general x1, matrix products, shards(): pre_act = jnp.dot(hidden_low, win_full, preferred_element_type=jnp.float32)  20.7 us
  transfers between devices with their start and end apart: 17, of which 9 were waited for; matrix products, arithmetic and copies ran while one was open for 29% of the time, Pallas kernels for 0%

commit v1 on v0

--- a/solution.py
+++ b/solution.py
@@ -238,12 +238,20 @@
             concat_axis=2,
             tiled=True,
         ),
-        lax.all_to_all(
-            grad_v.astype(jnp.bfloat16).reshape(seq_count, full_len, head_group * HEAD),
-            "seq",
-            split_axis=1,
-            concat_axis=2,
-            tiled=True,
+        jnp.concatenate(
+            lax.all_to_all(
+                jnp.stack(
+                    jnp.split(
+                        grad_v.astype(jnp.bfloat16).reshape(seq_count, full_len, head_group * HEAD),
+                        lax.axis_size("seq"),
+                        axis=1,
+                    )
+                ),
+                "seq",
+                0,
+                0,
+            ),
+            axis=2,
         ),
     )
     grad_q_rows = grad_q_tok.reshape(row_count, model_width)

time: 711 us -> 705 us (level)
  transfers between devices with their start and end apart: 17 -> 17, of which waited for: 9 -> 9; matrix products, arithmetic and copies ran while one was open for 29% -> 28% of each run, Pallas kernels for 0% -> 0%
where the time goes in v1:
time: 705 us; the launch traced here: 698 us
  waiting for transfers between devices  316 us (45%)
  matrix products  157 us (22%)
  blocking collectives  108 us (15%)
  local copies, waits for them, and re-layouts  53.4 us (8%)
  other arithmetic  31.6 us (4%)
  between operations  16.4 us (2%)
  starting transfers between devices  16.1 us (2%)
    reduce_scatter x1, waiting for transfers between devices, shards(): lax.psum_scatter(grad_win, 'dp', scatter_dimension=1, tiled=True)  99.1 us
    reduce_scatter x1, waiting for transfers between devices, shards(): lax.psum_scatter(grad_wout, 'dp', scatter_dimension=1, tiled=True)  97.9 us
    unnamed x2, blocking collectives  42 us
    all_gather x1, waiting for transfers between devices, shards(): lax.all_gather(w_key, 'dp', axis=1, tiled=True)  24.6 us
    dot_general x6, matrix products, row_product(): lax.dot_general(left, right, (((0,), (0,)), ((), ())), preferred_element_...  23.1 us
    all_gather x1, waiting for transfers between devices, shards(): lax.all_gather(w_out, 'dp', axis=1, tiled=True)  21.4 us
    psum x1, waiting for transfers between devices, shards(): lax.psum(share_wq.astype(jnp.bfloat16), 'seq').astype(jnp.float32)  20.8 us
    dot_general x1, matrix products, shards(): pre_act = jnp.dot(hidden_low, win_full, preferred_element_type=jnp.float32)  20.7 us
  transfers between devices with their start and end apart: 17, of which 9 were waited for; matrix products, arithmetic and copies ran while one was open for 28% of the time, Pallas kernels for 0%

profile of v1, /device:TPU:0, one launch (start us, length us, event | category | flops | bytes accessed | tf_op | source)
XLA Modules:
  0.0 698.4 jit_solution(14039726795966619966)
XLA Ops:
  10.6 24.6 %all-gather.7.cloned.1.call-done = bf16[768,768]{0,1:T(8,128)(2,1)} async-done(((bf16[768,96]{0,1:T(8,128)(2,1)}), bf16[768,768]{0,1:T(8,128)(2,1)}) %all-gather.7.cloned.1.call-update) | async-done | bytes 1179664 | tf_op jit(solution)/shard_map/all_gather | solution.py:116
  43.5 15.9 %all-gather.11.cloned.1.call-done = bf16[768,768]{0,1:T(8,128)(2,1)} async-done(((bf16[768,96]{0,1:T(8,128)(2,1)}), bf16[768,768]{0,1:T(8,128)(2,1)}) %all-gather.11.cloned.1.call-update) | async-done | bytes 1179664 | tf_op jit(solution)/shard_map/all_gather | solution.py:115
  63.3 4.2 all-to-all-start.2
  69.8 16.1 %all-reduce.9 = (bf16[768]{0:T(1024)(128)(2,1)S(1)}, bf16[768]{0:T(1024)(128)(2,1)S(1)}, bf16[768]{0:T(1024)(128)(2,1)S(1)}, bf16[768]{0:T(1024)(128)(2,1)S(1)}) all-reduce(bf16[768]{0:T(1024)(128)(2,1)S(1)} %dynamic-update-slice.1, bf16[768]{0:T(1024)(128)(2,1)S(1)} %dynamic-update-slice, ...), channel_id=1, replica_groups=mesh['seq'=4,'dp'=8] {'dp'}, use_global_device_ids=true, to_apply=%add.1 | all-reduce | flops 3072 | bytes 12288
  91.9 4.4 all-to-all-start.1
  111.0 7.3 %fusion.20 = f32[2,1024,3,256]{1,3,2,0:T(8,128)S(1)} fusion(f32[2,1024,3,64]{1,3,2,0:T(8,128)S(1)} %reshape.236, f32[64,256]{1,0:T(8,128)S(1)} %copy-done), kind=kOutput, calls=%fused_computation.64 | convolution fusion | flops 1208352768 | bytes 7929856 | tf_op jit(solution)/shard_map/snhe,em->snhm/dot_general | solution.py:38
  118.4 7.2 %fusion.16 = (f32[2,3,256]{2,1,0:T(4,128)S(1)}, f32[2,1024,3,256]{3,1,2,0:T(8,128)S(1)}) fusion(f32[2,1024]{1,0:T(2,128)S(1)} %compare_convert_fusion, f32[2,1024,3]{1,2,0:T(4,128)S(1)} %broadcast_multiply_fusion.3, f32[64,256]{1,0:T(8,128)S(1)} %copy-done, f32[2,1024,3,64]{1,3,2,0:T(8,128)S(1)} %reshape.235), kind=kOutput, calls=%fused_computation.31 | convolution fusion | flops 1213069824 | bytes 7968768 | tf_op jit(solution)/shard_map/snhe,em->snhm/dot_general | solution.py:38
  132.9 5.6 fusion.53
  144.6 12.5 %all-to-all-done.3 = bf16[2,1024,192]{2,0,1:T(2,128)(2,1)S(1)} async-done(((bf16[2,1024,192]{2,0,1:T(2,128)(2,1)}), bf16[2,1024,192]{2,0,1:T(2,128)(2,1)S(1)}, u32[]{:S(2)}, u32[]{:S(2)}) %all-to-all-start.3) | async-done | bytes 786464 | tf_op jit(solution)/shard_map/all_to_all | solution.py:166
  169.2 20.7 %multiply_convert_fusion = (bf16[512,3072]{1,0:T(8,128)(2,1)}, f32[512,3072]{1,0:T(8,128)}, f32[512,3072]{1,0:T(8,128)}) fusion(bf16[768,3072]{1,0:T(8,128)(2,1)} %all-gather.15.cloned.1.call-done, f32[512,768]{1,0:T(8,128)} %copy-done.21, f32[768]{0:T(1024)S(1)} %convert_element_type.205, f32[768]{0:T(1024)S(1)} %convert_element_type.204, ...), kind=kOutput, calls=%fused_computation.6 | convolution fusion | flops 2520121344 | bytes 22030336 | tf_op jit(solution)/shard_map/dot_general | solution.py:172
  190.0 21.4 %all-gather.17.cloned.1.call-done = bf16[3072,768]{0,1:T(8,128)(2,1)} async-done(((bf16[3072,96]{0,1:T(8,128)(2,1)}), bf16[3072,768]{0,1:T(8,128)(2,1)}) %all-gather.17.cloned.1.call-update) | async-done | bytes 4718608 | tf_op jit(solution)/shard_map/all_gather | solution.py:120
  211.4 6.6 fusion.55
  220.7 7.7 %add_convert_fusion = bf16[512,3072]{1,0:T(8,128)(2,1)S(1)} fusion(f32[512,3072]{1,0:T(8,128)S(1)} %copy-done.41, f32[512,3072]{1,0:T(8,128)} %get-tuple-element.56, bf16[3072,768]{0,1:T(8,128)(2,1)S(1)} %copy-done.33, f32[512,768]{1,0:T(8,128)S(1)} %get-tuple-element.40), kind=kOutput, calls=%fused_computation.5 | convolution fusion | flops 2438332416 | bytes 22020096 | tf_op jit(solution)/shard_map/dot_general | solution.py:199
  240.3 15.4 %all_to_all.92 = bf16[2,256,768]{1,0,2:T(2,128)(2,1)S(1)} all-to-all(bf16[2,256,768]{1,0,2:T(2,128)(2,1)S(1)} %copy.80), channel_id=1, replica_groups=mesh['seq'=4,'dp'=8] {'seq'}, dimensions={2} | all-to-all | bytes 1572864 | tf_op jit(solution)/shard_map/all_to_all | solution.py:215
  261.1 10.2 %fusion.8 = f32[2,3,256,64]{2,3,1,0:T(8,128)S(1)} fusion(f32[2,1024,3,256]{1,3,2,0:T(8,128)} %copy-done.1, f32[2,1024,3]{1,2,0:T(4,128)S(1)} %broadcast_multiply_fusion.2, f32[2,1024,3,64]{1,3,2,0:T(8,128)} %reshape.239, f32[2,1024,3]{1,2,0:T(4,128)S(1)} %bitcast.218), kind=kOutput, calls=%fused_computation.23 | convolution fusion | flops 1209925632 | bytes 8306688 | tf_op jit(solution)/shard_map/snhm,snhe->shme/dot_general | solution.py:80
  271.4 7.2 %fusion.24 = bf16[2,3,64,1024]{3,2,1,0:T(8,128)(2,1)S(1)} fusion(f32[2,3,256,64]{2,3,1,0:T(8,128)S(1)} %fusion.8, f32[2,1024,3,256]{3,1,2,0:T(8,128)S(1)} %bitcast.171, f32[2,1024]{1,0:T(2,128)S(1)} %compare_convert_fusion, f32[2,1024,3]{1,2,0:T(4,128)S(1)} %broadcast_multiply_fusion.3), kind=kOutput, calls=%fused_computation.74 | convolution fusion | flops 1211498496 | bytes 7503872 | tf_op jit(solution)/shard_map/snhm,shme->snhe/dot_general | solution.py:88
  281.0 13.0 %all_to_all.93 = bf16[4,2,256,192]{2,1,3,0:T(2,128)(2,1)S(1)} all-to-all(bf16[4,2,256,192]{2,1,3,0:T(2,128)(2,1)S(1)} %pad_maximum_fusion), channel_id=1, replica_groups=mesh['seq'=4,'dp'=8] {'seq'}, dimensions={0} | all-to-all | bytes 1572864 | tf_op jit(solution)/shard_map/all_to_all | solution.py:242
  299.8 8.4 %fusion.7 = f32[2,3,1,256]{3,2,1,0:T(1,128)S(1)} fusion(f32[2,1024,3,256]{1,3,2,0:T(8,128)} %copy-done.1, f32[2,1024,3]{1,2,0:T(4,128)S(1)} %broadcast_multiply_fusion.2, f32[2,1024,3,1]{1,2,0,3:T(4,128)S(1)} %bitcast.220), kind=kOutput, calls=%fused_computation.22 | convolution fusion | flops 20447232 | bytes 6346752 | tf_op jit(solution)/shard_map/snhm,snh->shm/dot_general | solution.py:81
  308.3 4.8 fusion.56
  313.1 6.2 multiply_convert_fusion.1
  320.2 14.7 %all_to_all.94 = bf16[2,1024,192]{2,0,1:T(2,128)(2,1)S(1)} all-to-all(bf16[2,1024,192]{2,0,1:T(2,128)(2,1)S(1)} %copy.89), channel_id=1, replica_groups=mesh['seq'=4,'dp'=8] {'seq'}, dimensions={1} | all-to-all | bytes 1572864 | tf_op jit(solution)/shard_map/all_to_all | solution.py:234
  341.2 11.6 %fusion.57 = (f32[2,1024,3]{1,2,0:T(4,128)S(1)}, f32[2,1024,3,256]{1,3,2,0:T(8,128)S(1)}) fusion(f32[2,1024,3,256]{1,3,2,0:T(8,128)} %copy-done.1, f32[2,1024,3]{1,2,0:T(4,128)S(1)} %broadcast_multiply_fusion.2, f32[2,3,256]{2,1,0:T(4,128)S(1)} %get-tuple-element.50, f32[2,1024,3]{1,2,0:T(4,128)S(1)} %negate_divide_fusion, ...), kind=kOutput, calls=%fused_computation.131 | convolution fusion | flops 1216210944 | bytes 14653440 | tf_op jit(solution)/shard_map/snhe,shme->snhm/dot_general | solution.py:77
  352.8 4.3 multiply_convert_fusion.2
  358.0 13.4 %all_to_all.95 = bf16[2,1024,192]{2,0,1:T(2,128)(2,1)S(1)} all-to-all(bf16[2,1024,192]{2,0,1:T(2,128)(2,1)S(1)} %copy.84), channel_id=1, replica_groups=mesh['seq'=4,'dp'=8] {'seq'}, dimensions={1} | all-to-all | bytes 1572864 | tf_op jit(solution)/shard_map/all_to_all | solution.py:227
  376.6 7.2 %fusion.46 = f32[768,3072]{1,0:T(8,128)} fusion(bf16[512,3072]{1,0:T(8,128)(2,1)} %copy-done.40, f32[512,768]{1,0:T(8,128)S(1)} %copy-done.23, f32[768]{0:T(1024)S(1)} %convert_element_type.205, f32[768]{0:T(1024)S(1)} %convert_element_type.204, f32[512]{0:T(512)S(1)} %add_rsqrt_fusion.1, f32[512]{0:T(512)S(1)} %broadcast_multiply_fusion.8), kind=kOutput, calls=%fused_computation.123 | convolution fusion | flops 2417885184 | bytes 14166016 | tf_op jit(solution)/shard_map/dot_general | solution.py:31
  385.2 7.0 %fusion.31 = f32[3072,768]{0,1:T(8,128)} fusion(bf16[512,3072]{1,0:T(8,128)(2,1)} %get-tuple-element.38, f32[512,768]{1,0:T(8,128)S(1)} %copy-done.20), kind=kOutput, calls=%fused_computation.84 | convolution fusion | flops 2416312320 | bytes 14155776 | tf_op jit(solution)/shard_map/dot_general | solution.py:31
  397.2 16.3 %reduce-scatter.7.cloned.1.call-done = f32[768,96]{0,1:T(8,128)} async-done(((f32[768,768]{0,1:T(8,128)}), f32[768,96]{0,1:T(8,128)}) %reduce-scatter.7.cloned.1.call-update) | async-done | bytes 294928 | tf_op jit(solution)/shard_map/reduce_scatter | solution.py:285
  415.1 99.1 %reduce-scatter.15.cloned.1.call-done = f32[768,384]{1,0:T(8,128)} async-done(((f32[768,3072]{1,0:T(8,128)}), f32[768,384]{1,0:T(8,128)}) %reduce-scatter.15.cloned.1.call-update) | async-done | bytes 1179664 | tf_op jit(solution)/shard_map/reduce_scatter | solution.py:289
  516.4 97.9 %reduce-scatter.17.cloned.1.call-done = f32[3072,96]{0,1:T(8,128)} async-done(((f32[3072,768]{0,1:T(8,128)}), f32[3072,96]{0,1:T(8,128)}) %reduce-scatter.17.cloned.1.call-update) | async-done | bytes 1179664 | tf_op jit(solution)/shard_map/reduce_scatter | solution.py:290
  617.1 25.9 %all-reduce.8 = (bf16[768]{0:T(1024)(128)(2,1)S(1)}, bf16[768]{0:T(1024)(128)(2,1)S(1)}, bf16[768]{0:T(1024)(128)(2,1)S(1)}, bf16[768]{0:T(1024)(128)(2,1)S(1)}) all-reduce(f32[768]{0:T(1024)S(1)} %get-tuple-element.12, f32[768]{0:T(1024)S(1)} %get-tuple-element.17, ...), channel_id=8, replica_groups=mesh['seq'=4,'dp'=8] {'dp'}, use_global_device_ids=true, to_apply=%region_27.0.clone | all-reduce | flops 3072 | bytes 18432
  643.4 9.9 %all-reduce.10 = (bf16[96]{0:T(256)(128)(2,1)S(1)}, bf16[96]{0:T(256)(128)(2,1)S(1)}, bf16[96]{0:T(256)(128)(2,1)S(1)}, bf16[96]{0:T(256)(128)(2,1)S(1)}) all-reduce(bf16[96]{0:T(256)(128)(2,1)S(1)} %dynamic-slice.19, bf16[96]{0:T(256)(128)(2,1)S(1)} %dynamic-slice.18, ...), channel_id=1, replica_groups=mesh['seq'=4,'dp'=8] {'seq'}, use_global_device_ids=true, to_apply=%region_28.0 | all-reduce | flops 384 | bytes 1536 | tf_op jit(solution)/shard_map/psum | solution.py:314
  661.0 20.8 %all-reduce.14.cloned.1.call-done = (bf16[768,96]{0,1:T(8,128)(2,1)}, bf16[768,96]{0,1:T(8,128)(2,1)}, bf16[768,96]{0,1:T(8,128)(2,1)}, bf16[768,96]{0,1:T(8,128...) async-done(((bf16[768,96]{0,1:T(8,128)(2,1)}, bf16[768,96]{0,1:T(8,128)(2,1)}, bf16[768,96]{0,1:T(8,128)(2,1)}, bf16[768,96]{0,1:T(8,128)(2,1)}, ...) | async-done | bytes 1769488 | tf_op jit(solution)/shard_map/psum | solution.py:308
  (250 shorter events, 134.3 us)
Async XLA Ops:
  7.2 103.8 %copy-start = (f32[64,256]{1,0:T(8,128)S(1)}, f32[64,256]{1,0:T(8,128)}, u32[]{:S(2)}) copy-start(f32[64,256]{1,0:T(8,128)} %param.16) | copy-start | bytes 196612
  7.2 28.0 %all-gather.7.cloned.1.call-start = ((), (), s32[]{:S(2)}) async-start(), calls=%async_computation.14 | async-start | bytes 1327104 | tf_op jit(solution)/shard_map/all_gather | solution.py:116
  7.9 51.4 %all-gather.11.cloned.1.call-start = ((), (), s32[]{:S(2)}) async-start(), calls=%async_computation.16 | async-start | bytes 1327104 | tf_op jit(solution)/shard_map/all_gather | solution.py:115
  8.7 77.2 %all-gather.9.cloned.1.call-start = ((), (), s32[]{:S(2)}) async-start(), calls=%async_computation.15 | async-start | bytes 1327104 | tf_op jit(solution)/shard_map/all_gather | solution.py:117
  9.4 155.8 %all-gather.13.cloned.1.call-start = ((), (), s32[]{:S(2)}) async-start(), calls=%async_computation.17 | async-start | bytes 1327104 | tf_op jit(solution)/shard_map/all_gather | solution.py:118
  10.0 159.2 %all-gather.15.cloned.1.call-start = ((), (), s32[]{:S(2)}) async-start(), calls=%async_computation.18 | async-start | bytes 5308416 | tf_op jit(solution)/shard_map/all_gather | solution.py:119
  37.5 21.9 %copy-start.12 = (bf16[2,256,768]{2,1,0:T(8,128)(2,1)S(1)}, bf16[2,256,768]{2,1,0:T(8,128)(2,1)}, u32[]{:S(2)}) copy-start(bf16[2,256,768]{2,1,0:T(8,128)(2,1)} %param.14) | copy-start | bytes 2359300
  39.3 24.0 %all-to-all-start = ((bf16[2,256,768]{1,0,2:T(2,128)(2,1)}), bf16[2,256,768]{1,0,2:T(2,128)(2,1)S(1)}, u32[]{:S(2)}, u32[]{:S(2)}) async-start(bf16[2,256,768]{1,0,2:T(2,128)(2,1)} %copy.67), calls=%async_computation | async-start | bytes 1572864 | tf_op jit(solution)/shard_map/all_to_all | solution.py:142
  42.9 168.6 %all-gather.17.cloned.1.call-start = ((), (), s32[]{:S(2)}) async-start(), calls=%async_computation.19 | async-start | bytes 5308416 | tf_op jit(solution)/shard_map/all_gather | solution.py:120
  63.3 28.6 %all-to-all-start.2 = ((bf16[2,256,768]{1,0,2:T(2,128)(2,1)}), bf16[2,256,768]{1,0,2:T(2,128)(2,1)}, u32[]{:S(2)}, u32[]{:S(2)}) async-start(bf16[2,256,768]{1,0,2:T(2,128)(2,1)} %copy.73), calls=%async_computation.2 | async-start | bytes 1572864 | tf_op jit(solution)/shard_map/all_to_all | solution.py:135
  91.9 26.5 %copy-start.3 = (f32[2,1024,3,64]{1,3,2,0:T(8,128)}, f32[2,1024,3,64]{1,3,2,0:T(8,128)S(1)}, u32[]{:S(2)}) copy-start(f32[2,1024,3,64]{1,3,2,0:T(8,128)S(1)} %reshape.235) | copy-start | bytes 4718596
  91.9 13.8 %all-to-all-start.1 = ((bf16[2,256,768]{1,0,2:T(2,128)(2,1)}), bf16[2,256,768]{1,0,2:T(2,128)(2,1)}, u32[]{:S(2)}, u32[]{:S(2)}) async-start(bf16[2,256,768]{1,0,2:T(2,128)(2,1)} %copy.70), calls=%async_computation.1 | async-start | bytes 1572864 | tf_op jit(solution)/shard_map/all_to_all | solution.py:149
  101.9 9.1 %copy-start.5 = (f32[2,1024,3,64]{1,3,2,0:T(8,128)}, f32[2,1024,3,64]{1,3,2,0:T(8,128)S(1)}, u32[]{:S(2)}) copy-start(f32[2,1024,3,64]{1,3,2,0:T(8,128)S(1)} %reshape.236) | copy-start | bytes 4718596
  118.4 14.5 %copy-start.1 = (f32[2,1024,3,256]{1,3,2,0:T(8,128)}, f32[2,1024,3,256]{1,3,2,0:T(8,128)S(1)}, u32[]{:S(2)}) copy-start(f32[2,1024,3,256]{1,3,2,0:T(8,128)S(1)} %fusion.20) | copy-start | bytes 18874372
  140.4 16.7 %all-to-all-start.3 = ((bf16[2,1024,192]{2,0,1:T(2,128)(2,1)}), bf16[2,1024,192]{2,0,1:T(2,128)(2,1)S(1)}, u32[]{:S(2)}, u32[]{:S(2)}) async-start(bf16[2,1024,192]{2,0,1:T(2,128)(2,1)} %copy.77), calls=%async_computation.3 | async-start | bytes 2097152 | tf_op jit(solution)/shard_map/all_to_all | solution.py:166
  144.0 248.3 %reduce-scatter.13.cloned.1.call-start = ((), (), s32[]{:S(2)}) async-start(), calls=%async_computation.23 | async-start | bytes 2654208 | tf_op jit(solution)/shard_map/reduce_scatter | solution.py:288
  211.4 9.3 %copy-start.41 = (f32[512,3072]{1,0:T(8,128)S(1)}, f32[512,3072]{1,0:T(8,128)}, u32[]{:S(2)}) copy-start(f32[512,3072]{1,0:T(8,128)} %get-tuple-element.39) | copy-start | bytes 18874372
  219.1 9.3 %slice-start.4 = ((s8[4718592]{0:T(1024)(128)(4,1)}), s8[4194304]{0:T(1024)(128)(4,1)S(1)}, s32[]{:S(2)}) async-start(s8[4718592]{0:T(1024)(128)(4,1)} %bitcast.226), calls=%async_computation.31 | async-start | bytes 8388608
  235.0 159.0 %reduce-scatter.11.cloned.1.call-start = ((), (), s32[]{:S(2)}) async-start(), calls=%async_computation.22 | async-start | bytes 2654208 | tf_op jit(solution)/shard_map/reduce_scatter | solution.py:287
  258.1 13.3 %slice-start = ((s8[6291456]{0:T(1024)(128)(4,1)}), s8[2097152]{0:T(1024)(128)(4,1)S(1)}, s32[]{:S(2)}) async-start(s8[6291456]{0:T(1024)(128)(4,1)} %bitcast.170), calls=%async_computation.27 | async-start | bytes 4194304
  261.1 10.2 %slice-start.1 = ((s8[6291456]{0:T(1024)(128)(4,1)}), s8[4194304]{0:T(1024)(128)(4,1)S(1)}, s32[]{:S(2)}) async-start(s8[6291456]{0:T(1024)(128)(4,1)} %bitcast.170), calls=%async_computation.28 | async-start | bytes 8388608
  279.5 15.6 %copy-start.14 = (bf16[2,256,768]{2,1,0:T(8,128)(2,1)S(1)}, bf16[2,256,768]{2,1,0:T(8,128)(2,1)}, u32[]{:S(2)}) copy-start(bf16[2,256,768]{2,1,0:T(8,128)(2,1)} %param.14) | copy-start | bytes 2359300
  295.1 13.2 %slice-start.2 = ((s8[6291456]{0:T(1024)(128)(4,1)}), s8[2097152]{0:T(1024)(128)(4,1)S(1)}, s32[]{:S(2)}) async-start(s8[6291456]{0:T(1024)(128)(4,1)} %bitcast.172), calls=%async_computation.29 | async-start | bytes 4194304
  297.3 98.3 %reduce-scatter.9.cloned.1.call-start = ((), (), s32[]{:S(2)}) async-start(), calls=%async_computation.21 | async-start | bytes 2654208 | tf_op jit(solution)/shard_map/reduce_scatter | solution.py:286
  297.4 10.9 %slice-start.3 = ((s8[6291456]{0:T(1024)(128)(4,1)}), s8[4194304]{0:T(1024)(128)(4,1)S(1)}, s32[]{:S(2)}) async-start(s8[6291456]{0:T(1024)(128)(4,1)} %bitcast.172), calls=%async_computation.30 | async-start | bytes 8388608
  341.1 11.7 %copy-start.6 = (f32[2,1024,3,64]{1,3,2,0:T(8,128)S(1)}, f32[2,1024,3,64]{1,3,2,0:T(8,128)}, u32[]{:S(2)}) copy-start(f32[2,1024,3,64]{1,3,2,0:T(8,128)} %copy-done.5) | copy-start | bytes 4718596
  341.1 72.4 %reduce-scatter.7.cloned.1.call-start = ((), (), s32[]{:S(2)}) async-start(), calls=%async_computation.20 | async-start | bytes 2654208 | tf_op jit(solution)/shard_map/reduce_scatter | solution.py:285
  376.5 137.7 %reduce-scatter.15.cloned.1.call-start = ((), (), s32[]{:S(2)}) async-start(), calls=%async_computation.24 | async-start | bytes 10616832 | tf_op jit(solution)/shard_map/reduce_scatter | solution.py:289
  383.9 230.4 %reduce-scatter.17.cloned.1.call-start = ((), (), s32[]{:S(2)}) async-start(), calls=%async_computation.25 | async-start | bytes 10616832 | tf_op jit(solution)/shard_map/reduce_scatter | solution.py:290
  392.2 289.5 %all-reduce.14.cloned.1.call-start = ((), (), s32[]{:S(2)}) async-start(), calls=%async_computation.26 | async-start | bytes 3538944 | tf_op jit(solution)/shard_map/psum | solution.py:308
  415.1 240.2 %copy-start.35 = (bf16[768,768]{0,1:T(8,128)(2,1)S(1)}, bf16[768,768]{0,1:T(8,128)(2,1)}, u32[]{:S(2)}) copy-start(bf16[768,768]{0,1:T(8,128)(2,1)} %all-gather.11.cloned.1.call-done) | copy-start | bytes 3538948
  681.8 8.8 %copy-start.30 = (bf16[3072,96]{0,1:T(8,128)(2,1)S(1)}, bf16[3072,96]{0,1:T(8,128)(2,1)}, u32[]{:S(2)}) copy-start(bf16[3072,96]{0,1:T(8,128)(2,1)} %get-tuple-element.37) | copy-start | bytes 1769476
  (33 other events, 130.0 us)
Sparse Core Ops, SparseCore 0:
  9.6 25.4 all-gather.6
  36.8 22.5 all-gather.10
  61.0 22.5 all-gather.8
  85.1 22.3 all-gather.12
  108.9 51.0 all-gather.14
  161.5 49.8 all-gather.16
  235.1 35.8 reduce-scatter.12
  297.4 34.2 reduce-scatter.10
  341.2 34.1 reduce-scatter.8
  377.6 35.9 reduce-scatter.6
  415.8 98.3 reduce-scatter.14
  516.4 97.8 reduce-scatter.16
  618.7 63.0 all-reduce.13
